TPU v7x, 512 devices: a whole 4x4x16 slice. The times are simulated.
512 devices in a mesh: tok: 64 (over y_lo, z, core), head: 8 (over y_hi, x).
Axes of the slice: x: 4, y: 4 (y_hi: 2, y_lo: 2; y = y_hi * 2 + y_lo), z: 16, core: 2. Of those that a mesh axis runs over, the one named last changes fastest.
Arguments:
- tokens: bfloat16 [8192, 3072], P('tok', 'head'), may hold values from -6 to 6
- norm_gain: bfloat16 [3072], replicated, may hold values from 0.099609375 to 1.8984375
- w_query: bfloat16 [3072, 3072], P('tok', 'head'), may hold values from -0.3125 to 0.3125
- w_key: bfloat16 [3072, 1024], P('tok', 'head'), may hold values from -0.3125 to 0.3125
- w_value: bfloat16 [3072, 1024], P('tok', 'head'), may hold values from -0.3125 to 0.3125
- w_out: bfloat16 [3072, 3072], P('tok', 'head'), may hold values from -0.109375 to 0.109375
- cache_keys: bfloat16 [64, 512, 1024], P(None, 'tok', 'head')
- cache_values: bfloat16 [64, 512, 1024], P(None, 'tok', 'head'), may hold values from -18 to 18
- lengths: int32 [64], P('tok'), may hold values from 2 to 512, as said below
- page_table: int32 [64, 32], P('tok'), may hold values from 0 to 31, each once within a row
Outputs:
- mixed: bfloat16 [8192, 3072], P('tok', 'head')
- decode_keys: bfloat16 [2048, 16, 1024], P('tok', None, 'head')
- decode_values: bfloat16 [2048, 16, 1024], P('tok', None, 'head')
Inputs may be any that keep to these rules, and one draw needn't show every extreme that they name: lengths are 2 or more, and some request has exactly 512. Each row of page_table names every page slot once.
All inputs are finite; a program needn't handle non-finite values.
Results may differ from a plain program's by a relative error of at most 0.018.
Values may be sent and summed in bfloat16 or wider, within the bound.
A program may use at most 64 MiB of HBM per device.

v0:
```python
import math

import jax
import jax.numpy as jnp
from jax import lax
from jax.sharding import PartitionSpec as P

HD = 128


rope_base = 500000.0
norm_eps = 1e-05


def rotate(values, positions, head_size):
    row_count = values.shape[0]
    shaped = values.reshape(row_count, -1, head_size)
    half_size = head_size // 2
    exponent = jnp.arange(half_size, dtype=jnp.float32) * (2.0 / head_size)
    frequency = jnp.exp(-math.log(rope_base) * exponent)
    angles = positions.astype(jnp.float32)[:, None] * frequency[None, :]
    cosine = jnp.cos(angles)[:, None, :]
    sine_part = jnp.sin(angles)[:, None, :]
    first_half = shaped[:, :, :half_size]
    second_half = shaped[:, :, half_size:]
    turned = jnp.concatenate(
        [
            first_half * cosine - second_half * sine_part,
            second_half * cosine + first_half * sine_part,
        ],
        axis=2,
    )
    return turned.reshape(row_count, -1)


def attend_head(queries, cached_keys, cached_values, span_keys, span_values, live_slots, causal):
    score_scale = 1.0 / math.sqrt(queries.shape[1])
    numbers = (((1,), (1,)), ((), ()))
    cached_scores = (
        lax.dot_general(queries, cached_keys, numbers, preferred_element_type=jnp.float32)
        * score_scale
    )
    span_scores = (
        lax.dot_general(queries, span_keys, numbers, preferred_element_type=jnp.float32)
        * score_scale
    )
    cached_scores = jnp.where(live_slots[None, :], cached_scores, -jnp.inf)
    span_scores = jnp.where(causal, span_scores, -jnp.inf)
    row_max = jnp.maximum(jnp.max(cached_scores, axis=1), jnp.max(span_scores, axis=1))[:, None]
    cached_exp = jnp.exp(cached_scores - row_max)
    span_exp = jnp.exp(span_scores - row_max)
    row_total = jnp.sum(cached_exp, axis=1, keepdims=True) + jnp.sum(
        span_exp, axis=1, keepdims=True
    )
    cached_weights = (cached_exp / row_total).astype(jnp.bfloat16)
    span_weights = (span_exp / row_total).astype(jnp.bfloat16)
    head_out = jnp.dot(cached_weights, cached_values, preferred_element_type=jnp.float32)
    head_out = head_out + jnp.dot(span_weights, span_values, preferred_element_type=jnp.float32)
    return head_out.astype(jnp.bfloat16)


def shards(
    tokens, norm_gain, w_query, w_key, w_value, w_out, cache_keys, cache_values, lengths, page_table
):
    full_rows = lax.all_gather(tokens, "head", axis=1, tiled=True)
    span_len = full_rows.shape[0]
    as_float = full_rows.astype(jnp.float32)
    mean_square = jnp.mean(as_float * as_float, axis=1, keepdims=True)
    normed = (
        as_float * lax.rsqrt(mean_square + norm_eps) * norm_gain.astype(jnp.float32)[None, :]
    ).astype(jnp.bfloat16)

    def add_rows(weight_rows):
        return jnp.dot(normed, weight_rows, preferred_element_type=jnp.float32)

    query_sum = add_rows(lax.all_gather(w_query, "tok", axis=0, tiled=True))
    key_sum = add_rows(lax.all_gather(w_key, "tok", axis=0, tiled=True))
    value_sum = add_rows(lax.all_gather(w_value, "tok", axis=0, tiled=True))
    length = lengths[0]
    positions = length + jnp.arange(span_len, dtype=jnp.int32)
    queries = rotate(query_sum, positions, HD).astype(jnp.bfloat16)
    key_new = rotate(key_sum, positions, HD).astype(jnp.bfloat16)
    value_new = value_sum.astype(jnp.bfloat16)
    moved_keys, moved_values = (
        lax.all_to_all(cache_keys, "tok", split_axis=0, concat_axis=1, tiled=True),
        lax.all_to_all(cache_values, "tok", split_axis=0, concat_axis=1, tiled=True),
    )
    slot_total = moved_keys.shape[1]
    live_slots = jnp.arange(slot_total, dtype=jnp.int32) < length
    keys_live = jnp.where(live_slots[:, None], moved_keys[0], jnp.zeros_like(moved_keys[0]))
    values_live = jnp.where(live_slots[:, None], moved_values[0], jnp.zeros_like(moved_values[0]))
    slot_count = page_table.shape[1]
    page_keys = keys_live.reshape(slot_count, -1, keys_live.shape[1])
    page_values = values_live.reshape(slot_count, -1, values_live.shape[1])
    decode_keys = jnp.zeros_like(page_keys).at[page_table[0]].set(page_keys)
    decode_values = jnp.zeros_like(page_values).at[page_table[0]].set(page_values)
    token_ids = jnp.arange(span_len, dtype=jnp.int32)
    causal = token_ids[None, :] <= token_ids[:, None]
    local_heads = queries.shape[1] // HD

    def one_head(head_number):
        head_start = head_number * HD
        return attend_head(
            lax.dynamic_slice_in_dim(queries, head_start, HD, 1),
            keys_live,
            values_live,
            key_new,
            value_new,
            live_slots,
            causal,
        )

    heads_out = lax.map(one_head, jnp.arange(local_heads, dtype=jnp.int32))
    attention = jnp.transpose(heads_out, (1, 0, 2)).reshape(span_len, local_heads * HD)
    partial_out = lax.dot_general(
        attention,
        lax.all_gather(w_out, "tok", axis=0, tiled=True),
        (((1,), (1,)), ((), ())),
        preferred_element_type=jnp.float32,
    )
    mixed = lax.psum_scatter(
        partial_out.astype(jnp.bfloat16), "head", scatter_dimension=1, tiled=True
    )
    return (mixed, decode_keys, decode_values)


def solution(mesh):
    in_specs = (
        P("tok", "head"),
        P(),
        P("tok", "head"),
        P("tok", "head"),
        P("tok", "head"),
        P("tok", "head"),
        P(None, "tok", "head"),
        P(None, "tok", "head"),
        P("tok"),
        P("tok", None),
    )
    out_specs = (P("tok", "head"), P("tok", None, "head"), P("tok", None, "head"))
    return jax.shard_map(shards, mesh=mesh, in_specs=in_specs, out_specs=out_specs, check_vma=False)
```

profile of v0, /device:TPU:1, one launch (start us, length us, event | category | flops | bytes accessed | tf_op | source)
XLA Modules:
  0.0 355.9 jit_solution(9091315769664037303)
XLA Ops:
  7.2 0.7 all-gather.3.cloned.1.call-update
  7.9 18.2 %all-to-all-start = ((bf16[64,8,128]{2,1,0:T(8,128)(2,1)}), bf16[64,8,128]{2,1,0:T(8,128)(2,1)S(1)}, u32[]{:S(2)}, u32[]{:S(2)}) async-start(bf16[64,8,128]{2,1,0:T(8,128)(2,1)} %param.18), calls=%async_computation | async-start | bytes 262144 | tf_op jit(solution)/shard_map/all_to_all | solution.py:85
  26.1 0.7 all-gather.5.cloned.1.call-update
  26.9 31.4 %all_gather.15 = bf16[128,3072]{1,0:T(8,128)(2,1)S(1)} all-gather(bf16[128,384]{1,0:T(8,128)(2,1)} %param.12), channel_id=1, replica_groups=mesh['tok'=64,'head'=8] {'head'}, dimensions={1}, use_global_device_ids=true | all-gather | bytes 884736 | tf_op jit(solution)/shard_map/all_gather | solution.py:65
  58.3 0.2 fusion.17
  59.2 70.1 %all_gather.17 = bf16[3072,128]{1,0:T(8,128)(2,1)S(1)} all-gather(bf16[48,128]{1,0:T(8,128)(2,1)S(1)} %copy-done.2), channel_id=1, replica_groups=mesh['tok'=64,'head'=8] {'tok'}, dimensions={0}, use_global_device_ids=true | all-gather | bytes 798720 | tf_op jit(solution)/shard_map/all_gather | solution.py:77
  129.4 0.5 convolution_bitcast_fusion
  130.1 61.7 %all_gather.18 = bf16[3072,128]{1,0:T(8,128)(2,1)S(1)} all-gather(bf16[48,128]{1,0:T(8,128)(2,1)S(1)} %copy-done.3), channel_id=1, replica_groups=mesh['tok'=64,'head'=8] {'tok'}, dimensions={0}, use_global_device_ids=true | all-gather | bytes 798720 | tf_op jit(solution)/shard_map/all_gather | solution.py:78
  191.8 4.2 %all-to-all-start.1 = ((bf16[64,8,128]{2,1,0:T(8,128)(2,1)}), bf16[64,8,128]{2,1,0:T(8,128)(2,1)S(1)}, u32[]{:S(2)}, u32[]{:S(2)}) async-start(bf16[64,8,128]{2,1,0:T(8,128)(2,1)} %param.19), calls=%async_computation.1 | async-start | bytes 262144 | tf_op jit(solution)/shard_map/all_to_all | solution.py:86
  196.5 0.4 convolution_convert_fusion.1
  196.9 17.1 %all-to-all-done.1 = bf16[64,8,128]{2,1,0:T(8,128)(2,1)S(1)} async-done(((bf16[64,8,128]{2,1,0:T(8,128)(2,1)}), bf16[64,8,128]{2,1,0:T(8,128)(2,1)S(1)}, u32[]{:S(2)}, u32[]{:S(2)}) %all-to-all-start.1) | async-done | bytes 131104 | tf_op jit(solution)/shard_map/all_to_all | solution.py:86
  214.2 2.8 fusion.31
  217.0 9.7 %while.11 = (s32[]{:T(128)}, bf16[3,128,128]{1,2,0:T(8,128)(2,1)S(1)}, s32[3]{0:T(128)S(1)}, bf16[128,384]{0,1:T(8,128)(2,1)S(1)}, bf16[512,128]{1,0:T(8,128)(2,...) while((s32[]{:T(128)}, ...), condition=%wide.region_6.7_spmd.clone, body=%wide.region_1.6_spmd.clone.sunk | while | flops 42647812 | bytes 1680583 | solution.py:113
  217.0 0.6 dynamic_slice.22
  218.3 0.7 iota_compare_fusion.4
  218.9 0.3 fusion.58
  219.7 0.3 fusion.62
  220.3 0.6 dynamic_slice.22
  221.5 0.7 iota_compare_fusion.4
  222.2 0.3 fusion.58
  222.9 0.3 fusion.62
  223.5 0.6 dynamic_slice.22
  224.8 0.7 iota_compare_fusion.4
  225.4 0.3 fusion.58
  226.2 0.3 fusion.62
  226.8 34.3 %all-gather.5.cloned.1.call-done = bf16[3072,384]{1,0:T(8,128)(2,1)} async-done(((bf16[48,384]{1,0:T(8,128)(2,1)}), bf16[3072,384]{1,0:T(8,128)(2,1)}) %all-gather.5.cloned.1.call-update) | async-done | bytes 2359312 | tf_op jit(solution)/shard_map/all_gather | solution.py:117
  261.0 2.5 convolution_convert_fusion
  263.6 1.2 copy.23
  265.0 1.5 scatter_fusion
  266.5 1.5 scatter_fusion.1
  268.1 79.6 %reduce-scatter.4.cloned.1.call-done = bf16[384,128]{1,0:T(8,128)(2,1)} async-done(((bf16[3072,128]{1,0:T(8,128)(2,1)}), bf16[384,128]{1,0:T(8,128)(2,1)}) %reduce-scatter.4.cloned.1.call-update) | async-done | bytes 98320
  347.7 1.6 copy.24
  (61 shorter events, 3.3 us)
Async XLA Ops:
  7.2 51.4 %copy-start.4 = (bf16[3072]{0:T(1024)(128)(2,1)S(1)}, bf16[3072]{0:T(1024)(128)(2,1)}, u32[]{:S(2)}) copy-start(bf16[3072]{0:T(1024)(128)(2,1)} %param.13) | copy-start | bytes 18436
  7.2 52.1 %copy-start.2 = (bf16[48,128]{1,0:T(8,128)(2,1)S(1)}, bf16[48,128]{1,0:T(8,128)(2,1)}, u32[]{:S(2)}) copy-start(bf16[48,128]{1,0:T(8,128)(2,1)} %param.15) | copy-start | bytes 36868
  7.2 207.0 %all-gather.3.cloned.1.call-start = ((), (), s32[]{:S(2)}) async-start(), calls=%async_computation.3 | async-start | bytes 2396160 | tf_op jit(solution)/shard_map/all_gather | solution.py:76
  7.9 183.9 %all-to-all-start = ((bf16[64,8,128]{2,1,0:T(8,128)(2,1)}), bf16[64,8,128]{2,1,0:T(8,128)(2,1)S(1)}, u32[]{:S(2)}, u32[]{:S(2)}) async-start(bf16[64,8,128]{2,1,0:T(8,128)(2,1)} %param.18), calls=%async_computation | async-start | bytes 262144 | tf_op jit(solution)/shard_map/all_to_all | solution.py:85
  26.1 234.9 %all-gather.5.cloned.1.call-start = ((), (), s32[]{:S(2)}) async-start(), calls=%async_computation.4 | async-start | bytes 2396160 | tf_op jit(solution)/shard_map/all_gather | solution.py:117
  58.5 71.6 %copy-start.3 = (bf16[48,128]{1,0:T(8,128)(2,1)S(1)}, bf16[48,128]{1,0:T(8,128)(2,1)}, u32[]{:S(2)}) copy-start(bf16[48,128]{1,0:T(8,128)(2,1)} %param.16) | copy-start | bytes 36868
  191.8 22.2 %all-to-all-start.1 = ((bf16[64,8,128]{2,1,0:T(8,128)(2,1)}), bf16[64,8,128]{2,1,0:T(8,128)(2,1)S(1)}, u32[]{:S(2)}, u32[]{:S(2)}) async-start(bf16[64,8,128]{2,1,0:T(8,128)(2,1)} %param.19), calls=%async_computation.1 | async-start | bytes 262144 | tf_op jit(solution)/shard_map/all_to_all | solution.py:86
  196.1 151.6 %reduce-scatter.4.cloned.1.call-start = ((), (), s32[]{:S(2)}) async-start(), calls=%async_computation.5 | async-start | bytes 884736
  263.6 1.2 copy-start.5
  266.5 82.8 %copy-start.1 = (bf16[32,16,128]{2,1,0:T(8,128)(2,1)}, bf16[32,16,128]{2,1,0:T(8,128)(2,1)S(1)}, u32[]{:S(2)}) copy-start(bf16[32,16,128]{2,1,0:T(8,128)(2,1)S(1)} %scatter_fusion) | copy-start | bytes 393220
  268.1 81.3 %copy-start = (bf16[32,16,128]{2,1,0:T(8,128)(2,1)}, bf16[32,16,128]{2,1,0:T(8,128)(2,1)S(1)}, u32[]{:S(2)}) copy-start(bf16[32,16,128]{2,1,0:T(8,128)(2,1)S(1)} %scatter_fusion.1) | copy-start | bytes 393220
Sparse Core Ops, SparseCore 0:
  10.2 128.7 all-gather.2
  141.1 119.8 all-gather.4
  265.5 82.1 reduce-scatter.3
where the time goes:
time: 357 us; the launch traced here: 356 us
  blocking collectives  163 us (46%)
  waiting for transfers between devices  132 us (37%)
  starting transfers between devices  22.5 us (6%)
  between operations  14.7 us (4%)
  matrix products  8.99 us (3%)
  local copies, waits for them, and re-layouts  8.13 us (2%)
  other arithmetic  3.71 us (1%)
    unnamed x4, waiting for transfers between devices  81 us
    all_gather x1, blocking collectives, shards(): key_sum = add_rows(lax.all_gather(w_key, 'tok', axis=0, tiled=True))  70.1 us
    all_gather x1, blocking collectives, shards(): value_sum = add_rows(lax.all_gather(w_value, 'tok', axis=0, tiled=True))  61.7 us
    all_gather x1, waiting for transfers between devices, shards(): lax.all_gather(w_out, 'tok', axis=0, tiled=True)  34.3 us
    all_gather x1, blocking collectives, shards(): full_rows = lax.all_gather(tokens, 'head', axis=1, tiled=True)  31.4 us
    all_to_all x1, starting transfers between devices, shards(): lax.all_to_all(cache_keys, 'tok', split_axis=0, concat_axis=1, tiled=True)  18.2 us
    all_to_all x1, waiting for transfers between devices, shards(): lax.all_to_all(cache_values, 'tok', split_axis=0, concat_axis=1, tiled=True)  17.1 us
  transfers between devices with their start and end apart: 5, of which 3 were waited for; matrix products, arithmetic and copies ran while one was open for 4% of the time, Pallas kernels for 0%

commit v1 on v0

v1 whole, which is shorter than its diff:
```python
import functools
import math

import jax
import jax.numpy as jnp
from jax import lax
from jax.experimental import pallas as pl
from jax.experimental.pallas import tpu as pltpu
from jax.sharding import PartitionSpec as P

MESH = pl.DeviceIdType.MESH
HD = 128
NZ = 16
rope_base = 500000.0
norm_eps = 1e-05
NT = (((1,), (1,)), ((), ()))


def kernel(
    n_tok, n_head,
    len_ref, inv_ref, gain_ref, tok_in, wq_in, wk_in, wv_in, wo_in, ck_in, cv_in,
    mixed_ref, dk_ref, dv_ref,
    buf_t, buf_q, buf_kv, buf_o, buf_ck, buf_cv, normed, live_k, live_v, part_send, part_recv,
    own_sem, t_recv, q_recv, kv_recv, o_recv, c_recv, p_recv,
    t_send, w_send, c_send, p_send,
):
    me_t = lax.axis_index("tok")
    me_h = lax.axis_index("head")
    yl = me_t // (2 * NZ)
    z = lax.rem(me_t // 2, NZ)
    core = lax.rem(me_t, 2)
    yl_other = 1 - yl

    def tok_id(y, zz, c):
        return y * (2 * NZ) + lax.rem(zz + NZ, NZ) * 2 + c

    right = tok_id(yl, z + 1, core)
    left = tok_id(yl, z - 1, core)
    across = tok_id(yl_other, z, core)
    twin = tok_id(yl, z, 1 - core)

    own = [
        pltpu.make_async_copy(tok_in, buf_t.at[me_h], own_sem.at[0]),
        pltpu.make_async_copy(wq_in, buf_q.at[me_t], own_sem.at[1]),
        pltpu.make_async_copy(wk_in, buf_kv.at[me_t, :, pl.ds(0, HD)], own_sem.at[2]),
        pltpu.make_async_copy(wv_in, buf_kv.at[me_t, :, pl.ds(HD, HD)], own_sem.at[3]),
        pltpu.make_async_copy(wo_in, buf_o.at[me_t], own_sem.at[4]),
        pltpu.make_async_copy(ck_in.at[me_t], buf_ck.at[me_t], own_sem.at[5]),
        pltpu.make_async_copy(cv_in.at[me_t], buf_cv.at[me_t], own_sem.at[6]),
    ]
    for copy in own:
        copy.start()

    barrier = pltpu.get_barrier_semaphore()

    @pl.loop(1, n_tok)
    def _(i):
        pl.semaphore_signal(
            barrier, inc=1, device_id={"tok": lax.rem(me_t + i, n_tok)}, device_id_type=MESH
        )

    @pl.loop(1, n_head)
    def _(i):
        pl.semaphore_signal(
            barrier, inc=1, device_id={"head": lax.rem(me_h + i, n_head)}, device_id_type=MESH
        )

    for copy in own:
        copy.wait()
    pl.semaphore_wait(barrier, n_tok + n_head - 2)

    y_hi = me_h // 4
    x = lax.rem(me_h, 4)
    far_head = (1 - y_hi) * 4 + x

    def send_tokens(slot, target):
        pltpu.make_async_remote_copy(
            src_ref=buf_t.at[slot], dst_ref=buf_t.at[slot], send_sem=t_send,
            recv_sem=t_recv.at[slot], device_id={"head": target}, device_id_type=MESH,
        ).start()

    send_tokens(me_h, far_head)
    for i in (1, 3, 2):
        send_tokens(me_h, y_hi * 4 + lax.rem(x + i, 4))

    streams = {
        "q": (buf_q, q_recv, w_send.at[0], "zy"),
        "kv": (buf_kv, kv_recv, w_send.at[1], "yz"),
        "o": (buf_o, o_recv, w_send.at[2], "zy"),
    }

    def send(name, slot, target):
        buf, recv, sem, _ = streams[name]
        pltpu.make_async_remote_copy(
            src_ref=buf.at[slot], dst_ref=buf.at[slot], send_sem=sem,
            recv_sem=recv.at[slot], device_id={"tok": target}, device_id_type=MESH,
        ).start()

    def arrived(name, slot):
        buf, recv, _, _ = streams[name]
        pltpu.make_async_copy(buf.at[slot], buf.at[slot], recv.at[slot]).wait()

    def send_cache(first, last):
        @pl.loop(first, last)
        def _(i):
            peer = lax.rem(me_t + i, n_tok)
            for number, (source, target) in enumerate(((ck_in, buf_ck), (cv_in, buf_cv))):
                pltpu.make_async_remote_copy(
                    src_ref=source.at[peer], dst_ref=target.at[me_t], send_sem=c_send.at[number],
                    recv_sem=c_recv.at[number], device_id={"tok": peer}, device_id_type=MESH,
                ).start()

    half = NZ // 2
    order = ("q", "kv", "o")

    def start_stream(name):
        mode = streams[name][3]
        send(name, me_t, across)
        send(name, me_t, right)
        send(name, me_t, left)
        send(name, me_t, twin)

    def second_start(name):
        if streams[name][3] == "yz":
            arrived(name, across)
            send(name, across, right)
            send(name, across, left)
            send(name, across, twin)

    def hop(name, step):
        mode = streams[name][3]
        rows = (yl,) if mode == "zy" else (yl, yl_other)
        for y in rows:
            slot = tok_id(y, z - step, core)
            arrived(name, slot)
            if step < half:
                send(name, slot, right)
            if mode == "zy":
                send(name, slot, across)
            send(name, slot, twin)
            if step < half:
                slot = tok_id(y, z + step, core)
                arrived(name, slot)
                if step < half - 1:
                    send(name, slot, left)
                if mode == "zy":
                    send(name, slot, across)
                send(name, slot, twin)

    def across_arrivals(name, step):
        if streams[name][3] != "zy":
            return
        slots = [tok_id(yl_other, z - step, core)]
        if 0 < step < half:
            slots.append(tok_id(yl_other, z + step, core))
        for slot in slots:
            arrived(name, slot)
            send(name, slot, twin)

    for name in order:
        start_stream(name)
    for name in order:
        second_start(name)
    send_cache(1, 8)
    for step in range(1, half + 1):
        for name in order:
            hop(name, step)
            across_arrivals(name, step - 1)
        if step == 1:
            pltpu.make_async_copy(buf_t.at[far_head], buf_t.at[far_head], t_recv.at[far_head]).wait()
            for i in (1, 3, 2):
                send_tokens(far_head, y_hi * 4 + lax.rem(x + i, 4))
        if step < half:
            send_cache(step * 8, step * 8 + 8)
    for name in order:
        across_arrivals(name, half)

    for i in range(1, 4):
        for y in range(2):
            slot = y * 4 + lax.rem(x + i, 4)
            pltpu.make_async_copy(buf_t.at[slot], buf_t.at[slot], t_recv.at[slot]).wait()
    rows = tok_in.shape[0]
    width = tok_in.shape[1]
    total = jnp.zeros((rows, 1), jnp.float32)
    for h in range(n_head):
        part = buf_t[h].astype(jnp.float32)
        total += jnp.sum(part * part, axis=1, keepdims=True)
    scale = lax.rsqrt(total / (n_head * width) + norm_eps)
    for h in range(n_head):
        gain = gain_ref[:, h * width:(h + 1) * width].astype(jnp.float32)
        normed[h] = (buf_t[h].astype(jnp.float32) * scale * gain).astype(jnp.bfloat16)

    length = len_ref[0]
    for number, (buf, live, out) in enumerate(((buf_ck, live_k, dk_ref), (buf_cv, live_v, dv_ref))):
        pltpu.make_async_copy(
            buf.at[pl.ds(0, n_tok - 1)], buf.at[pl.ds(0, n_tok - 1)], c_recv.at[number]
        ).wait()
        entries = buf[...].astype(jnp.float32)
        slots, head_size = entries.shape[0] * entries.shape[1], entries.shape[2]
        entries = entries.reshape(slots, head_size)
        slot_ids = lax.broadcasted_iota(jnp.int32, (slots, head_size), 0)
        entries = jnp.where(slot_ids < length, entries, 0.0)
        live[...] = entries.reshape(live.shape).astype(jnp.bfloat16)
        for page in range(out.shape[0]):
            out[page] = live[inv_ref[page]]

    for name in order:
        for y in range(2):
            for zz in range(NZ):
                arrived(name, tok_id(y, zz, 1 - core))

    group = n_tok // n_head
    depth = buf_q.shape[1]
    q_sum = jnp.zeros((rows, buf_q.shape[2]), jnp.float32)
    kv_sum = jnp.zeros((rows, buf_kv.shape[2]), jnp.float32)
    for h in range(n_head):
        lhs = normed[h]
        wq = buf_q[pl.ds(h * group, group)].reshape(group * depth, buf_q.shape[2])
        wkv = buf_kv[pl.ds(h * group, group)].reshape(group * depth, buf_kv.shape[2])
        q_sum += jnp.dot(lhs, wq, preferred_element_type=jnp.float32)
        kv_sum += jnp.dot(lhs, wkv, preferred_element_type=jnp.float32)

    lane = lax.broadcasted_iota(jnp.int32, (rows, HD), 1)
    row = lax.broadcasted_iota(jnp.int32, (rows, HD), 0)
    exponent = lax.rem(lane, HD // 2).astype(jnp.float32) * (2.0 / HD)
    frequency = jnp.exp(-math.log(rope_base) * exponent)
    angles = (row + length).astype(jnp.float32) * frequency
    cosine = jnp.cos(angles)
    sine = jnp.sin(angles)
    sine = jnp.where(lane < HD // 2, -sine, sine)

    def rope(v):
        return (v * cosine + pltpu.roll(v, HD // 2, 1) * sine).astype(jnp.bfloat16)

    key_new = rope(kv_sum[:, :HD])
    value_new = kv_sum[:, HD:].astype(jnp.bfloat16)
    keys = live_k[...].reshape(n_tok * buf_ck.shape[1], HD)
    values = live_v[...].reshape(n_tok * buf_ck.shape[1], HD)
    score_scale = 1.0 / math.sqrt(HD)
    cached_ids = lax.broadcasted_iota(jnp.int32, (rows, keys.shape[0]), 1)
    causal = lax.broadcasted_iota(jnp.int32, (rows, rows), 1) <= lax.broadcasted_iota(
        jnp.int32, (rows, rows), 0
    )
    heads_out = []
    for head in range(q_sum.shape[1] // HD):
        query = rope(q_sum[:, head * HD:(head + 1) * HD])
        cached = lax.dot_general(query, keys, NT, preferred_element_type=jnp.float32) * score_scale
        span = lax.dot_general(query, key_new, NT, preferred_element_type=jnp.float32) * score_scale
        cached = jnp.where(cached_ids < length, cached, -jnp.inf)
        span = jnp.where(causal, span, -jnp.inf)
        top = jnp.maximum(
            jnp.max(cached, axis=1, keepdims=True), jnp.max(span, axis=1, keepdims=True)
        )
        cached = jnp.exp(cached - top)
        span = jnp.exp(span - top)
        whole = jnp.sum(cached, axis=1, keepdims=True) + jnp.sum(span, axis=1, keepdims=True)
        out = jnp.dot((cached / whole).astype(jnp.bfloat16), values, preferred_element_type=jnp.float32)
        out += jnp.dot((span / whole).astype(jnp.bfloat16), value_new, preferred_element_type=jnp.float32)
        heads_out.append(out.astype(jnp.bfloat16))
    attention = jnp.concatenate(heads_out, axis=1)

    def partial_block(g):
        block = buf_o[pl.ds(g * group, group)].reshape(group * depth, buf_o.shape[2])
        return lax.dot_general(
            attention, block, NT, preferred_element_type=jnp.float32
        ).astype(jnp.bfloat16)

    def part_copy(i):
        return pltpu.make_async_remote_copy(
            src_ref=part_send.at[i - 1], dst_ref=part_recv.at[i - 1], send_sem=p_send.at[i - 1],
            recv_sem=p_recv.at[i - 1], device_id={"head": lax.rem(me_h + i, n_head)},
            device_id_type=MESH,
        )

    offsets = (4, 6, 2, 5, 3, 7, 1)
    for i in offsets:
        part_send[i - 1] = partial_block(lax.rem(me_h + i, n_head))
        part_copy(i).start()
    mixed = partial_block(me_h).astype(jnp.float32)
    for i in offsets[::-1]:
        part_copy(i).wait_recv()
        mixed += part_recv[i - 1].astype(jnp.float32)
    mixed_ref[...] = mixed.astype(jnp.bfloat16)

    for i in offsets:
        part_copy(i).wait_send()
    pltpu.make_async_copy(
        buf_t.at[pl.ds(0, n_head - 1)], buf_t.at[pl.ds(0, n_head - 1)], t_send
    ).wait()
    for number, buf in enumerate((buf_ck, buf_cv)):
        pltpu.make_async_copy(
            buf.at[pl.ds(0, n_tok - 1)], buf.at[pl.ds(0, n_tok - 1)], c_send.at[number]
        ).wait()
    for name in order:
        buf, _, sem, _ = streams[name]
        pltpu.make_async_copy(
            buf.at[pl.ds(0, n_tok - 1)], buf.at[pl.ds(0, n_tok - 1)], sem
        ).wait()


def solution(mesh):
    n_tok, n_head = mesh.shape["tok"], mesh.shape["head"]

    def shards(tokens, gain, w_query, w_key, w_value, w_out, cache_keys, cache_values, lengths, page_table):
        rows, width = tokens.shape
        pages = page_table.shape[1]
        depth, head_cols = w_query.shape
        page_ids = jnp.arange(pages, dtype=jnp.int32)
        inverse = jnp.sum(
            jnp.where(page_table[0][:, None] == page_ids[None, :], page_ids[:, None], 0), axis=0
        ).astype(jnp.int32)
        page_size = n_tok * cache_keys.shape[1] // pages
        paged = (pages, page_size, cache_keys.shape[2])
        bf16 = jnp.bfloat16
        dma = pltpu.SemaphoreType.DMA
        hbm = pl.BlockSpec(memory_space=pl.ANY)
        vmem = pl.BlockSpec(memory_space=pltpu.VMEM)
        smem = pl.BlockSpec(memory_space=pltpu.SMEM)
        return pl.pallas_call(
            functools.partial(kernel, n_tok, n_head),
            out_shape=(
                jax.ShapeDtypeStruct((rows, width), bf16),
                jax.ShapeDtypeStruct(paged, bf16),
                jax.ShapeDtypeStruct(paged, bf16),
            ),
            in_specs=[smem, smem, vmem] + [hbm] * 7,
            out_specs=(vmem, vmem, vmem),
            scratch_shapes=[
                pltpu.VMEM((n_head, rows, width), bf16),
                pltpu.VMEM((n_tok, depth, head_cols), bf16),
                pltpu.VMEM((n_tok, depth, 2 * HD), bf16),
                pltpu.VMEM((n_tok, depth, head_cols), bf16),
                pltpu.VMEM((n_tok,) + cache_keys.shape[1:], bf16),
                pltpu.VMEM((n_tok,) + cache_keys.shape[1:], bf16),
                pltpu.VMEM((n_head, rows, width), bf16),
                pltpu.VMEM(paged, bf16),
                pltpu.VMEM(paged, bf16),
                pltpu.VMEM((n_head - 1, rows, width), bf16),
                pltpu.VMEM((n_head - 1, rows, width), bf16),
                dma((7,)),
                dma((n_head,)),
                dma((n_tok,)),
                dma((n_tok,)),
                dma((n_tok,)),
                dma((2,)),
                dma((n_head - 1,)),
                dma,
                dma((3,)),
                dma((2,)),
                dma((n_head - 1,)),
            ],
            compiler_params=pltpu.CompilerParams(collective_id=0, has_side_effects=True),
        )(lengths, inverse, gain[None, :], tokens, w_query, w_key, w_value, w_out, cache_keys, cache_values)

    in_specs = (
        P("tok", "head"), P(), P("tok", "head"), P("tok", "head"), P("tok", "head"),
        P("tok", "head"), P(None, "tok", "head"), P(None, "tok", "head"), P("tok"), P("tok", None),
    )
    out_specs = (P("tok", "head"), P("tok", None, "head"), P("tok", None, "head"))
    return jax.shard_map(shards, mesh=mesh, in_specs=in_specs, out_specs=out_specs, check_vma=False)
```

time: 357 us -> 88.1 us (0.25)
  blocking collectives: 163 us -> 0 us
  waiting for transfers between devices: 132 us -> 0 us
  Pallas kernels: 0 us -> 80.8 us
  starting transfers between devices: 22.5 us -> 0 us
  between operations: 14.7 us -> 1.3 us
  matrix products: 8.99 us -> 0 us
    all_gather x3 -> x0, blocking collectives: 163 us -> none  [the longest x1 70.1 us: shards(): key_sum = add_rows(lax.all_gather(w_key, 'tok', axis=0, tiled=True))]
    unnamed x4 -> x0, waiting for transfers between devices: 81 us -> none
    pallas_call x0 -> x1, Pallas kernels: none -> 80.8 us  [shards(): pl.pallas_call(functools.partial(kernel, n_tok, n_head), out_shape=(jax.S...]
    all_gather x2 -> x0, waiting for transfers between devices: 34.3 us -> none  [the longest x1 34.3 us: shards(): lax.all_gather(w_out, 'tok', axis=0, tiled=True)]
    all_to_all x2 -> x0, starting transfers between devices: 22.4 us -> none  [the longest x1 18.2 us: shards(): lax.all_to_all(cache_keys, 'tok', split_axis=0, concat_axis=1, tiled=True)]
    all_to_all x2 -> x0, waiting for transfers between devices: 17.1 us -> none  [the longest x1 17.1 us: shards(): lax.all_to_all(cache_values, 'tok', split_axis=0, concat_axis=1, tiled=True)]
    dot_general x16 -> x0, matrix products: 8.99 us -> none  [the longest x3 3.68 us: add_rows(): return jnp.dot(normed, weight_rows, preferred_element_type=jnp.float32)]
  transfers between devices with their start and end apart: 5 -> 0, of which waited for: 3 -> 0; matrix products, arithmetic and copies ran while one was open for 4% -> 0% of each run, Pallas kernels for 0% -> 0%
where the time goes in v1:
time: 88.1 us; the launch traced here: 87.9 us
  Pallas kernels  80.8 us (92%)
  local copies, waits for them, and re-layouts  5.13 us (6%)
  between operations  1.3 us (1%)
    pallas_call x1, Pallas kernels, shards(): pl.pallas_call(functools.partial(kernel, n_tok, n_head), out_shape=(jax.S...  80.8 us
    unnamed x9, local copies, waits for them, and re-layouts  3.84 us

profile of v1, /device:TPU:1, one launch (start us, length us, event | category | flops | bytes accessed | tf_op | source)
XLA Modules:
  0.0 87.9 jit_solution(180647000538484838)
XLA Ops:
  1.3 0.0 copy-start.2
  1.3 0.6 copy-done.2
  1.9 0.6 select_reduce_fusion.inv_ref
  2.5 1.3 %broadcast_in_dim.19.gain_ref = bf16[1,3072]{1,0:T(2,128)(2,1)} reshape(bf16[3072]{0:T(1024)(128)(2,1)} %param.11) | data formatting | bytes 12288 | tf_op jit(solution)/shard_map/broadcast_in_dim | solution.py:353
  3.8 80.8 %shard_map.121 = (bf16[128,384]{1,0:T(8,128)(2,1)}, bf16[32,16,128]{2,1,0:T(8,128)(2,1)}, bf16[32,16,128]{2,1,0:T(8,128)(2,1)}) custom-call(s32[1]{0:T(128)S(6)} %copy.16.len_ref, s32[32]{0:T(128)} %select_reduce_fusion.inv_ref, bf16[1,3072]{1,0:T(2,128)(2,1)} %broadcast_in_dim.19.gain_ref, bf16[128,384]{1,0:T(8,128)(2,1)} %tok_in.1, bf16[48,384]{1,0:T(8,128)(2,1)} %wq_in.1, ...), custom_call_target="tpu_custom_call" | custom-call | tf_op jit(solution)/shard_map/pallas_call | solution.py:319
  84.7 0.0 copy-start.1
  84.7 1.6 %copy.17 = bf16[128,384]{1,0:T(8,128)(2,1)} copy(bf16[128,384]{1,0:T(8,128)(2,1)} %get-tuple-element.6) | data formatting | bytes 196608
  86.2 0.0 copy-done.1
  86.2 0.0 copy-start
  86.2 0.7 copy.18
  86.9 0.3 copy-done
  87.2 0.7 copy.19
Async XLA Ops:
  1.3 0.7 copy-start.2
  84.7 1.6 %copy-start.1 = (bf16[32,16,128]{2,1,0:T(8,128)(2,1)S(1)}, bf16[32,16,128]{2,1,0:T(8,128)(2,1)}, u32[]{:S(2)}) copy-start(bf16[32,16,128]{2,1,0:T(8,128)(2,1)} %get-tuple-element.7) | copy-start | bytes 393220
  86.2 1.0 %copy-start = (bf16[32,16,128]{2,1,0:T(8,128)(2,1)S(1)}, bf16[32,16,128]{2,1,0:T(8,128)(2,1)}, u32[]{:S(2)}) copy-start(bf16[32,16,128]{2,1,0:T(8,128)(2,1)} %get-tuple-element.8) | copy-start | bytes 393220

commit v2 on v1

v2 whole, which is shorter than its diff:
```python
import functools
import math

import jax
import jax.numpy as jnp
from jax import lax
from jax.experimental import pallas as pl
from jax.experimental.pallas import tpu as pltpu
from jax.sharding import PartitionSpec as P

MESH = pl.DeviceIdType.MESH
HD = 128
NZ = 16
LAG = 4
rope_base = 500000.0
norm_eps = 1e-05
NT = (((1,), (1,)), ((), ()))


def kernel(
    n_tok, n_head,
    len_ref, page_ref, gain_ref, tok_in, wq_in, wk_in, wv_in, wo_in, ck_in, cv_in,
    mixed_ref, dk_ref, dv_ref,
    buf_t, buf_q, buf_kv, buf_o, buf_ck, buf_cv, normed, live_k, live_v, part_send, part_recv,
    q_s, kv_s, cos_s, sin_s, att_s, inv_s,
    own_sem, t_recv, q_recv, kv_recv, o_recv, c_recv, p_recv,
    t_send, w_send, c_send, p_send,
):
    me_t = lax.axis_index("tok")
    me_h = lax.axis_index("head")
    yl = me_t // (2 * NZ)
    z = lax.rem(me_t // 2, NZ)
    core = lax.rem(me_t, 2)
    yl_other = 1 - yl
    y_hi = me_h // 4
    x = lax.rem(me_h, 4)
    y_far = 1 - y_hi
    far_head = y_far * 4 + x
    rows, width = tok_in.shape

    def tok_id(y, zz, c):
        return y * (2 * NZ) + lax.rem(zz + NZ, NZ) * 2 + c

    def head_id(y, i):
        return y * 4 + lax.rem(x + i, 4)

    right = tok_id(yl, z + 1, core)
    left = tok_id(yl, z - 1, core)
    across = tok_id(yl_other, z, core)
    twin = tok_id(yl, z, 1 - core)

    own = [
        pltpu.make_async_copy(wq_in, buf_q.at[me_t], own_sem.at[0]),
        pltpu.make_async_copy(wk_in, buf_kv.at[me_t, :, pl.ds(0, HD)], own_sem.at[1]),
        pltpu.make_async_copy(wv_in, buf_kv.at[me_t, :, pl.ds(HD, HD)], own_sem.at[2]),
        pltpu.make_async_copy(tok_in, buf_t.at[me_h], own_sem.at[3]),
        pltpu.make_async_copy(wo_in, buf_o.at[me_t], own_sem.at[4]),
        pltpu.make_async_copy(ck_in.at[me_t], buf_ck.at[me_t], own_sem.at[5]),
        pltpu.make_async_copy(cv_in.at[me_t], buf_cv.at[me_t], own_sem.at[6]),
    ]
    for copy in own:
        copy.start()

    barrier = pltpu.get_barrier_semaphore()
    for target in (right, left, across, twin):
        pl.semaphore_signal(barrier, inc=1, device_id={"tok": target}, device_id_type=MESH)
    for target in (head_id(y_hi, 1), head_id(y_hi, 2), head_id(y_hi, 3), far_head):
        pl.semaphore_signal(barrier, inc=1, device_id={"head": target}, device_id_type=MESH)

    length = len_ref[0]
    lane = lax.broadcasted_iota(jnp.int32, (rows, HD), 1)
    row = lax.broadcasted_iota(jnp.int32, (rows, HD), 0)
    exponent = lax.rem(lane, HD // 2).astype(jnp.float32) * (2.0 / HD)
    frequency = jnp.exp(-math.log(rope_base) * exponent)
    angles = (row + length).astype(jnp.float32) * frequency
    sine = jnp.sin(angles)
    cos_s[...] = jnp.cos(angles)
    sin_s[...] = jnp.where(lane < HD // 2, -sine, sine)

    for copy in own:
        copy.wait()
    pl.semaphore_wait(barrier, 8)

    def send_tokens(slot, target):
        pltpu.make_async_remote_copy(
            src_ref=buf_t.at[slot], dst_ref=buf_t.at[slot], send_sem=t_send,
            recv_sem=t_recv.at[slot], device_id={"head": target}, device_id_type=MESH,
        ).start()

    def tokens_arrived(slot):
        pltpu.make_async_copy(buf_t.at[slot], buf_t.at[slot], t_recv.at[slot]).wait()

    streams = {
        "q": (buf_q, q_recv, w_send.at[0], "zy"),
        "kv": (buf_kv, kv_recv, w_send.at[1], "yz"),
        "o": (buf_o, o_recv, w_send.at[2], "zy"),
    }

    def send(name, slot, target):
        buf, recv, sem, _ = streams[name]
        pltpu.make_async_remote_copy(
            src_ref=buf.at[slot], dst_ref=buf.at[slot], send_sem=sem,
            recv_sem=recv.at[slot], device_id={"tok": target}, device_id_type=MESH,
        ).start()

    def arrived(name, slot):
        buf, recv, _, _ = streams[name]
        pltpu.make_async_copy(buf.at[slot], buf.at[slot], recv.at[slot]).wait()

    def send_cache(peer):
        for number, (source, target) in enumerate(((ck_in, buf_ck), (cv_in, buf_cv))):
            pltpu.make_async_remote_copy(
                src_ref=source.at[peer], dst_ref=target.at[me_t], send_sem=c_send.at[number],
                recv_sem=c_recv.at[number], device_id={"tok": peer}, device_id_type=MESH,
            ).start()

    half = NZ // 2

    def at_step(y, step, c):
        if step == 0:
            return [tok_id(y, z, c)]
        slots = [tok_id(y, z - step, c)]
        return slots + [tok_id(y, z + step, c)] if step < half else slots

    def start_stream(name):
        send(name, me_t, across)
        send(name, me_t, right)
        send(name, me_t, left)
        send(name, me_t, twin)

    def second_start(name):
        arrived(name, across)
        send(name, across, right)
        send(name, across, left)
        send(name, across, twin)

    def hop(name, step):
        mode = streams[name][3]
        for y in (yl,) if mode == "zy" else (yl, yl_other):
            for number, slot in enumerate(at_step(y, step, core)):
                arrived(name, slot)
                if step < half - number:
                    send(name, slot, left if number else right)
                if mode == "zy":
                    send(name, slot, across)
                send(name, slot, twin)

    def across_arrivals(name, step):
        for slot in at_step(yl_other, step, core):
            arrived(name, slot)
            send(name, slot, twin)

    start_stream("q")
    start_stream("kv")
    send_tokens(me_h, far_head)
    for i in (1, 3, 2):
        send_tokens(me_h, head_id(y_hi, i))
    second_start("kv")
    send_cache(twin)

    @pl.loop(0, page_ref.shape[1])
    def _(slot):
        page = jnp.int32(0)
        for p in range(page_ref.shape[1]):
            page = jnp.where(page_ref[0, p] == slot, jnp.int32(p), page)
        inv_s[slot] = page

    def cache_step(step):
        if step <= half:
            for slot in at_step(yl, step, core):
                send_cache(slot)
        if 1 <= step <= half + 1:
            for slot in at_step(yl_other, step - 1, core):
                send_cache(slot)
            if step == 1:
                arrived("q", twin)
            if step >= 2:
                for slot in at_step(yl, step - 1, 1 - core):
                    arrived("q", slot)
                    send_cache(slot)
        if step >= 2:
            for slot in at_step(yl_other, step - 2, 1 - core):
                arrived("q", slot)
                send_cache(slot)

    def square_sum():
        for slot in [head_id(y_hi, i) for i in (1, 2, 3)] + [head_id(y_far, i) for i in (1, 2, 3)]:
            tokens_arrived(slot)
        total = jnp.zeros((rows, 1), jnp.float32)
        for h in range(n_head):
            part = buf_t[h].astype(jnp.float32)
            total += jnp.sum(part * part, axis=1, keepdims=True)
        return lax.rsqrt(total / (n_head * width) + norm_eps)

    def normalise(scale):
        for h in range(n_head):
            gain = gain_ref[pl.ds(h * width, width)].astype(jnp.float32)[None, :]
            normed[h] = (buf_t[h].astype(jnp.float32) * scale * gain).astype(jnp.bfloat16)

    group = n_tok // n_head
    depth = buf_q.shape[1]

    def project():
        for y in range(2):
            for zz in range(NZ):
                arrived("kv", tok_id(y, zz, 1 - core))
        q_sum = jnp.zeros(q_s.shape, jnp.float32)
        kv_sum = jnp.zeros(kv_s.shape, jnp.float32)
        for h in range(n_head):
            lhs = normed[h]
            wq = buf_q[pl.ds(h * group, group)].reshape(group * depth, buf_q.shape[2])
            wkv = buf_kv[pl.ds(h * group, group)].reshape(group * depth, buf_kv.shape[2])
            q_sum += jnp.dot(lhs, wq, preferred_element_type=jnp.float32)
            kv_sum += jnp.dot(lhs, wkv, preferred_element_type=jnp.float32)

        def rope(v):
            return (v * cos_s[...] + pltpu.roll(v, HD // 2, 1) * sin_s[...]).astype(jnp.bfloat16)

        for head in range(q_s.shape[1] // HD):
            q_s[:, head * HD:(head + 1) * HD] = rope(q_sum[:, head * HD:(head + 1) * HD])
        kv_s[:, :HD] = rope(kv_sum[:, :HD])
        kv_s[:, HD:] = kv_sum[:, HD:].astype(jnp.bfloat16)

    def page_caches():
        for number, (buf, live, out) in enumerate(((buf_ck, live_k, dk_ref), (buf_cv, live_v, dv_ref))):
            pltpu.make_async_copy(
                buf.at[pl.ds(0, n_tok - 1)], buf.at[pl.ds(0, n_tok - 1)], c_recv.at[number]
            ).wait()
            entries = buf[...].astype(jnp.float32)
            slots, head_size = entries.shape[0] * entries.shape[1], entries.shape[2]
            entries = entries.reshape(slots, head_size)
            slot_ids = lax.broadcasted_iota(jnp.int32, (slots, head_size), 0)
            entries = jnp.where(slot_ids < length, entries, 0.0)
            live[...] = entries.reshape(live.shape).astype(jnp.bfloat16)
            for page in range(out.shape[0]):
                out[page] = live[inv_s[page]]

    def attend(head):
        columns = slice(head * HD, (head + 1) * HD)
        keys = live_k[...].reshape(n_tok * buf_ck.shape[1], HD)
        values = live_v[...].reshape(n_tok * buf_ck.shape[1], HD)
        score_scale = 1.0 / math.sqrt(HD)
        cached_ids = lax.broadcasted_iota(jnp.int32, (rows, keys.shape[0]), 1)
        causal = lax.broadcasted_iota(jnp.int32, (rows, rows), 1) <= lax.broadcasted_iota(
            jnp.int32, (rows, rows), 0
        )
        query = q_s[:, columns]
        cached = lax.dot_general(query, keys, NT, preferred_element_type=jnp.float32) * score_scale
        span = lax.dot_general(query, kv_s[:, :HD], NT, preferred_element_type=jnp.float32) * score_scale
        cached = jnp.where(cached_ids < length, cached, -jnp.inf)
        span = jnp.where(causal, span, -jnp.inf)
        top = jnp.maximum(
            jnp.max(cached, axis=1, keepdims=True), jnp.max(span, axis=1, keepdims=True)
        )
        cached = jnp.exp(cached - top)
        span = jnp.exp(span - top)
        whole = jnp.sum(cached, axis=1, keepdims=True) + jnp.sum(span, axis=1, keepdims=True)
        out = jnp.dot((cached / whole).astype(jnp.bfloat16), values, preferred_element_type=jnp.float32)
        out += jnp.dot((span / whole).astype(jnp.bfloat16), kv_s[:, HD:], preferred_element_type=jnp.float32)
        att_s[:, columns] = out.astype(jnp.bfloat16)

    heads = q_s.shape[1] // HD
    scale = None
    for step in range(1, half + LAG + 1):
        if step <= half:
            hop("q", step)
            across_arrivals("q", step - 1)
            hop("kv", step)
        if step == half + 1:
            across_arrivals("q", half)
        if step == LAG:
            start_stream("o")
        if step > LAG:
            hop("o", step - LAG)
            across_arrivals("o", step - LAG - 1)
        if step <= half + 2:
            cache_step(step)
        if step == 1:
            tokens_arrived(far_head)
            for i in (1, 3, 2):
                send_tokens(far_head, head_id(y_hi, i))
        if step == half - 1:
            scale = square_sum()
            normalise(scale)
        if step == half + 2:
            project()
        if step == half + 3:
            page_caches()
            attend(0)
        if step == half + 4:
            for head in range(1, heads):
                attend(head)
    across_arrivals("o", half)
    for y in range(2):
        for zz in range(NZ):
            arrived("o", tok_id(y, zz, 1 - core))

    def partial_block(g):
        block = buf_o[pl.ds(g * group, group)].reshape(group * depth, buf_o.shape[2])
        return lax.dot_general(att_s[...], block, NT, preferred_element_type=jnp.float32)

    def part_copy(slot, target):
        return pltpu.make_async_remote_copy(
            src_ref=part_send.at[slot], dst_ref=part_recv.at[slot], send_sem=p_send.at[slot],
            recv_sem=p_recv.at[slot], device_id={"head": target}, device_id_type=MESH,
        )

    copies = [part_copy(i - 1, head_id(y_hi, i)) for i in (1, 2, 3)]
    copies += [part_copy(i + 2, head_id(y_hi, i)) for i in (1, 2, 3)]
    copies += [part_copy(6, far_head)]
    for i in (2, 1, 3):
        part_send[i - 1] = partial_block(head_id(y_far, i)).astype(jnp.bfloat16)
        copies[i - 1].start()
    far_sum = partial_block(far_head)
    for i in (2, 1, 3):
        part_send[i + 2] = partial_block(head_id(y_hi, i)).astype(jnp.bfloat16)
        copies[i + 2].start()
    for i in (1, 3, 2):
        copies[i - 1].wait_recv()
        far_sum += part_recv[i - 1].astype(jnp.float32)
    part_send[6] = far_sum.astype(jnp.bfloat16)
    copies[6].start()
    mixed = partial_block(me_h)
    for i in (1, 3, 2):
        copies[i + 2].wait_recv()
        mixed += part_recv[i + 2].astype(jnp.float32)
    copies[6].wait_recv()
    mixed_ref[...] = (mixed + part_recv[6].astype(jnp.float32)).astype(mixed_ref.dtype)

    for copy in copies:
        copy.wait_send()
    pltpu.make_async_copy(
        buf_t.at[pl.ds(0, n_head - 1)], buf_t.at[pl.ds(0, n_head - 1)], t_send
    ).wait()
    for number, buf in enumerate((buf_ck, buf_cv)):
        pltpu.make_async_copy(
            buf.at[pl.ds(0, n_tok - 1)], buf.at[pl.ds(0, n_tok - 1)], c_send.at[number]
        ).wait()
    for buf, _, sem, _ in streams.values():
        pltpu.make_async_copy(
            buf.at[pl.ds(0, n_tok - 1)], buf.at[pl.ds(0, n_tok - 1)], sem
        ).wait()


def solution(mesh):
    n_tok, n_head = mesh.shape["tok"], mesh.shape["head"]

    def shards(tokens, gain, w_query, w_key, w_value, w_out, cache_keys, cache_values, lengths, page_table):
        rows, width = tokens.shape
        pages = page_table.shape[1]
        depth, head_cols = w_query.shape
        page_size = n_tok * cache_keys.shape[1] // pages
        paged = (pages, page_size, cache_keys.shape[2])
        bf16 = jnp.bfloat16
        dma = pltpu.SemaphoreType.DMA
        hbm = pl.BlockSpec(memory_space=pl.ANY)
        vmem = pl.BlockSpec(memory_space=pltpu.VMEM)
        smem = pl.BlockSpec(memory_space=pltpu.SMEM)
        return pl.pallas_call(
            functools.partial(kernel, n_tok, n_head),
            out_shape=(
                jax.ShapeDtypeStruct((rows, width), bf16),
                jax.ShapeDtypeStruct(paged, bf16),
                jax.ShapeDtypeStruct(paged, bf16),
            ),
            in_specs=[smem, smem, vmem] + [hbm] * 7,
            out_specs=(vmem, vmem, vmem),
            scratch_shapes=[
                pltpu.VMEM((n_head, rows, width), bf16),
                pltpu.VMEM((n_tok, depth, head_cols), bf16),
                pltpu.VMEM((n_tok, depth, 2 * HD), bf16),
                pltpu.VMEM((n_tok, depth, head_cols), bf16),
                pltpu.VMEM((n_tok,) + cache_keys.shape[1:], bf16),
                pltpu.VMEM((n_tok,) + cache_keys.shape[1:], bf16),
                pltpu.VMEM((n_head, rows, width), bf16),
                pltpu.VMEM(paged, bf16),
                pltpu.VMEM(paged, bf16),
                pltpu.VMEM((n_head - 1, rows, width), bf16),
                pltpu.VMEM((n_head - 1, rows, width), bf16),
                pltpu.VMEM((rows, head_cols), bf16),
                pltpu.VMEM((rows, 2 * HD), bf16),
                pltpu.VMEM((rows, HD), jnp.float32),
                pltpu.VMEM((rows, HD), jnp.float32),
                pltpu.VMEM((rows, head_cols), bf16),
                pltpu.SMEM((pages,), jnp.int32),
                dma((7,)),
                dma((n_head,)),
                dma((n_tok,)),
                dma((n_tok,)),
                dma((n_tok,)),
                dma((2,)),
                dma((n_head - 1,)),
                dma,
                dma((3,)),
                dma((2,)),
                dma((n_head - 1,)),
            ],
            compiler_params=pltpu.CompilerParams(collective_id=0, has_side_effects=True),
        )(lengths, page_table, gain, tokens, w_query, w_key, w_value, w_out, cache_keys, cache_values)

    in_specs = (
        P("tok", "head"), P(), P("tok", "head"), P("tok", "head"), P("tok", "head"),
        P("tok", "head"), P(None, "tok", "head"), P(None, "tok", "head"), P("tok"), P("tok", None),
    )
    out_specs = (P("tok", "head"), P("tok", None, "head"), P("tok", None, "head"))
    return jax.shard_map(shards, mesh=mesh, in_specs=in_specs, out_specs=out_specs, check_vma=False)
```

time: 88.1 us -> 84.5 us (0.959)
  local copies, waits for them, and re-layouts: 5.13 us -> 3.19 us
  Pallas kernels: 80.8 us -> 79.7 us
    broadcast_in_dim x1 -> x0, local copies, waits for them, and re-layouts: 1.3 us -> none  [shards(): gain[None, :]]
    pallas_call x1, Pallas kernels: 80.8 us -> 79.7 us  [shards(): pl.pallas_call(functools.partial(kernel, n_tok, n_head), out_shape=(jax.S...]
    unnamed x9 -> x7, local copies, waits for them, and re-layouts: 3.84 us -> 3.19 us
where the time goes in v2:
time: 84.5 us; the launch traced here: 84.2 us
  Pallas kernels  79.7 us (94%)
  local copies, waits for them, and re-layouts  3.19 us (4%)
  between operations  1.3 us (2%)
    pallas_call x1, Pallas kernels, shards(): pl.pallas_call(functools.partial(kernel, n_tok, n_head), out_shape=(jax.S...  79.7 us
    unnamed x7, local copies, waits for them, and re-layouts  3.19 us

profile of v2, /device:TPU:1, one launch (start us, length us, event | category | flops | bytes accessed | tf_op | source)
XLA Modules:
  0.0 84.2 jit_solution(14350762955753951448)
XLA Ops:
  1.3 79.7 %shard_map.121 = (bf16[128,384]{1,0:T(8,128)(2,1)}, bf16[32,16,128]{2,1,0:T(8,128)(2,1)}, bf16[32,16,128]{2,1,0:T(8,128)(2,1)}) custom-call(s32[1]{0:T(128)S(6)} %copy.16.len_ref, s32[1,32]{1,0:T(1,128)} %page_ref.1, bf16[3072]{0:T(1024)(128)(2,1)} %gain_ref.1, bf16[128,384]{1,0:T(8,128)(2,1)} %tok_in.1, bf16[48,384]{1,0:T(8,128)(2,1)} %wq_in.1, ...), custom_call_target="tpu_custom_call" | custom-call | tf_op jit(solution)/shard_map/pallas_call | solution.py:359
  81.0 0.0 copy-start.1
  81.0 1.6 %copy.17 = bf16[128,384]{1,0:T(8,128)(2,1)} copy(bf16[128,384]{1,0:T(8,128)(2,1)} %get-tuple-element.6) | data formatting | bytes 196608
  82.6 0.0 copy-done.1
  82.6 0.0 copy-start
  82.6 0.7 copy.18
  83.3 0.3 copy-done
  83.6 0.7 copy.19
Async XLA Ops:
  81.0 1.6 %copy-start.1 = (bf16[32,16,128]{2,1,0:T(8,128)(2,1)S(1)}, bf16[32,16,128]{2,1,0:T(8,128)(2,1)}, u32[]{:S(2)}) copy-start(bf16[32,16,128]{2,1,0:T(8,128)(2,1)} %get-tuple-element.7) | copy-start | bytes 393220
  82.6 1.0 %copy-start = (bf16[32,16,128]{2,1,0:T(8,128)(2,1)S(1)}, bf16[32,16,128]{2,1,0:T(8,128)(2,1)}, u32[]{:S(2)}) copy-start(bf16[32,16,128]{2,1,0:T(8,128)(2,1)} %get-tuple-element.8) | copy-start | bytes 393220

commit v3 on v2

--- a/solution.py
+++ b/solution.py
@@ -11,7 +11,10 @@
 MESH = pl.DeviceIdType.MESH
 HD = 128
 NZ = 16
-LAG = 4
+LAG = 1
+GAP = 2
+LAST = max(LAG, 3)
+MODE_Q, MODE_KV, MODE_O = "zy", "yz", "zy"
 rope_base = 500000.0
 norm_eps = 1e-05
 NT = (((1,), (1,)), ((), ()))
@@ -21,7 +24,7 @@
     n_tok, n_head,
     len_ref, page_ref, gain_ref, tok_in, wq_in, wk_in, wv_in, wo_in, ck_in, cv_in,
     mixed_ref, dk_ref, dv_ref,
-    buf_t, buf_q, buf_kv, buf_o, buf_ck, buf_cv, normed, live_k, live_v, part_send, part_recv,
+    buf_t, buf_q, buf_kv, buf_o, buf_in, buf_c, normed, live_k, live_v, part_send, part_recv,
     q_s, kv_s, cos_s, sin_s, att_s, inv_s,
     own_sem, t_recv, q_recv, kv_recv, o_recv, c_recv, p_recv,
     t_send, w_send, c_send, p_send,
@@ -55,8 +58,10 @@
         pltpu.make_async_copy(wv_in, buf_kv.at[me_t, :, pl.ds(HD, HD)], own_sem.at[2]),
         pltpu.make_async_copy(tok_in, buf_t.at[me_h], own_sem.at[3]),
         pltpu.make_async_copy(wo_in, buf_o.at[me_t], own_sem.at[4]),
-        pltpu.make_async_copy(ck_in.at[me_t], buf_ck.at[me_t], own_sem.at[5]),
-        pltpu.make_async_copy(cv_in.at[me_t], buf_cv.at[me_t], own_sem.at[6]),
+        pltpu.make_async_copy(ck_in, buf_in.at[:, 0], own_sem.at[5]),
+        pltpu.make_async_copy(cv_in, buf_in.at[:, 1], own_sem.at[6]),
+        pltpu.make_async_copy(ck_in.at[me_t], buf_c.at[me_t, 0], own_sem.at[7]),
+        pltpu.make_async_copy(cv_in.at[me_t], buf_c.at[me_t, 1], own_sem.at[8]),
     ]
     for copy in own:
         copy.start()
@@ -91,9 +96,9 @@
         pltpu.make_async_copy(buf_t.at[slot], buf_t.at[slot], t_recv.at[slot]).wait()
 
     streams = {
-        "q": (buf_q, q_recv, w_send.at[0], "zy"),
-        "kv": (buf_kv, kv_recv, w_send.at[1], "yz"),
-        "o": (buf_o, o_recv, w_send.at[2], "zy"),
+        "q": (buf_q, q_recv, w_send.at[0], MODE_Q),
+        "kv": (buf_kv, kv_recv, w_send.at[1], MODE_KV),
+        "o": (buf_o, o_recv, w_send.at[2], MODE_O),
     }
 
     def send(name, slot, target):
@@ -108,11 +113,10 @@
         pltpu.make_async_copy(buf.at[slot], buf.at[slot], recv.at[slot]).wait()
 
     def send_cache(peer):
-        for number, (source, target) in enumerate(((ck_in, buf_ck), (cv_in, buf_cv))):
-            pltpu.make_async_remote_copy(
-                src_ref=source.at[peer], dst_ref=target.at[me_t], send_sem=c_send.at[number],
-                recv_sem=c_recv.at[number], device_id={"tok": peer}, device_id_type=MESH,
-            ).start()
+        pltpu.make_async_remote_copy(
+            src_ref=buf_in.at[peer], dst_ref=buf_c.at[me_t], send_sem=c_send,
+            recv_sem=c_recv, device_id={"tok": peer}, device_id_type=MESH,
+        ).start()
 
     half = NZ // 2
 
@@ -129,12 +133,15 @@
         send(name, me_t, twin)
 
     def second_start(name):
+        if streams[name][3] == "zy":
+            return
         arrived(name, across)
         send(name, across, right)
         send(name, across, left)
         send(name, across, twin)
 
-    def hop(name, step):
+    def forward(name, step):
+        rest = []
         mode = streams[name][3]
         for y in (yl,) if mode == "zy" else (yl, yl_other):
             for number, slot in enumerate(at_step(y, step, core)):
@@ -142,21 +149,30 @@
                 if step < half - number:
                     send(name, slot, left if number else right)
                 if mode == "zy":
-                    send(name, slot, across)
-                send(name, slot, twin)
+                    rest.append((name, slot, across))
+                rest.append((name, slot, twin))
+        return rest
 
     def across_arrivals(name, step):
         for slot in at_step(yl_other, step, core):
-            arrived(name, slot)
-            send(name, slot, twin)
+            if streams[name][3] == "zy":
+                arrived(name, slot)
+                send(name, slot, twin)
+            if name == "q":
+                send_cache(slot)
+
+    def twin_arrivals(y, step):
+        for slot in at_step(y, step, 1 - core):
+            arrived("q", slot)
+            send_cache(slot)
 
     start_stream("q")
     start_stream("kv")
     send_tokens(me_h, far_head)
     for i in (1, 3, 2):
         send_tokens(me_h, head_id(y_hi, i))
+    second_start("q")
     second_start("kv")
-    send_cache(twin)
 
     @pl.loop(0, page_ref.shape[1])
     def _(slot):
@@ -164,24 +180,6 @@
         for p in range(page_ref.shape[1]):
             page = jnp.where(page_ref[0, p] == slot, jnp.int32(p), page)
         inv_s[slot] = page
-
-    def cache_step(step):
-        if step <= half:
-            for slot in at_step(yl, step, core):
-                send_cache(slot)
-        if 1 <= step <= half + 1:
-            for slot in at_step(yl_other, step - 1, core):
-                send_cache(slot)
-            if step == 1:
-                arrived("q", twin)
-            if step >= 2:
-                for slot in at_step(yl, step - 1, 1 - core):
-                    arrived("q", slot)
-                    send_cache(slot)
-        if step >= 2:
-            for slot in at_step(yl_other, step - 2, 1 - core):
-                arrived("q", slot)
-                send_cache(slot)
 
     def square_sum():
         for slot in [head_id(y_hi, i) for i in (1, 2, 3)] + [head_id(y_far, i) for i in (1, 2, 3)]:
@@ -222,11 +220,11 @@
         kv_s[:, HD:] = kv_sum[:, HD:].astype(jnp.bfloat16)
 
     def page_caches():
-        for number, (buf, live, out) in enumerate(((buf_ck, live_k, dk_ref), (buf_cv, live_v, dv_ref))):
-            pltpu.make_async_copy(
-                buf.at[pl.ds(0, n_tok - 1)], buf.at[pl.ds(0, n_tok - 1)], c_recv.at[number]
-            ).wait()
-            entries = buf[...].astype(jnp.float32)
+        pltpu.make_async_copy(
+            buf_c.at[pl.ds(0, n_tok - 1)], buf_c.at[pl.ds(0, n_tok - 1)], c_recv
+        ).wait()
+        for number, (live, out) in enumerate(((live_k, dk_ref), (live_v, dv_ref))):
+            entries = buf_c[:, number].astype(jnp.float32)
             slots, head_size = entries.shape[0] * entries.shape[1], entries.shape[2]
             entries = entries.reshape(slots, head_size)
             slot_ids = lax.broadcasted_iota(jnp.int32, (slots, head_size), 0)
@@ -237,8 +235,8 @@
 
     def attend(head):
         columns = slice(head * HD, (head + 1) * HD)
-        keys = live_k[...].reshape(n_tok * buf_ck.shape[1], HD)
-        values = live_v[...].reshape(n_tok * buf_ck.shape[1], HD)
+        keys = live_k[...].reshape(n_tok * buf_c.shape[2], HD)
+        values = live_v[...].reshape(n_tok * buf_c.shape[2], HD)
         score_scale = 1.0 / math.sqrt(HD)
         cached_ids = lax.broadcasted_iota(jnp.int32, (rows, keys.shape[0]), 1)
         causal = lax.broadcasted_iota(jnp.int32, (rows, rows), 1) <= lax.broadcasted_iota(
@@ -260,37 +258,51 @@
         att_s[:, columns] = out.astype(jnp.bfloat16)
 
     heads = q_s.shape[1] // HD
-    scale = None
-    for step in range(1, half + LAG + 1):
+    waiting = []
+    for step in range(half + 1):
+        waiting.append((min(step + GAP, half + 1), functools.partial(across_arrivals, "q", step)))
+    for step in range(half + 1):
+        waiting.append((min(step + GAP, half + 1), functools.partial(twin_arrivals, yl, step)))
+        waiting.append((min(step + 2 * GAP, half + 1), functools.partial(twin_arrivals, yl_other, step)))
+        waiting.append((LAG + step + GAP, functools.partial(across_arrivals, "o", step)))
+    if LAG == 0:
+        start_stream("o")
+    for step in range(1, half + LAST + 1):
+        rest = []
         if step <= half:
-            hop("q", step)
-            across_arrivals("q", step - 1)
-            hop("kv", step)
-        if step == half + 1:
-            across_arrivals("q", half)
+            rest += forward("q", step)
+            rest += forward("kv", step)
+        if step == LAG + 1:
+            second_start("o")
+        if LAG < step <= half + LAG:
+            rest += forward("o", step - LAG)
         if step == LAG:
             start_stream("o")
-        if step > LAG:
-            hop("o", step - LAG)
-            across_arrivals("o", step - LAG - 1)
-        if step <= half + 2:
-            cache_step(step)
+        for name, slot, target in rest:
+            send(name, slot, target)
+        for due, action in waiting:
+            if due == step:
+                action()
+        if step <= half:
+            for slot in at_step(yl, step, core):
+                send_cache(slot)
         if step == 1:
             tokens_arrived(far_head)
             for i in (1, 3, 2):
                 send_tokens(far_head, head_id(y_hi, i))
         if step == half - 1:
-            scale = square_sum()
-            normalise(scale)
+            normalise(square_sum())
+        if step == half + 1:
+            project()
         if step == half + 2:
-            project()
-        if step == half + 3:
             page_caches()
             attend(0)
-        if step == half + 4:
+        if step == half + 3:
             for head in range(1, heads):
                 attend(head)
-    across_arrivals("o", half)
+    for due, action in waiting:
+        if due > half + LAST:
+            action()
     for y in range(2):
         for zz in range(NZ):
             arrived("o", tok_id(y, zz, 1 - core))
@@ -332,10 +344,9 @@
     pltpu.make_async_copy(
         buf_t.at[pl.ds(0, n_head - 1)], buf_t.at[pl.ds(0, n_head - 1)], t_send
     ).wait()
-    for number, buf in enumerate((buf_ck, buf_cv)):
-        pltpu.make_async_copy(
-            buf.at[pl.ds(0, n_tok - 1)], buf.at[pl.ds(0, n_tok - 1)], c_send.at[number]
-        ).wait()
+    pltpu.make_async_copy(
+        buf_c.at[pl.ds(0, n_tok - 1)], buf_c.at[pl.ds(0, n_tok - 1)], c_send
+    ).wait()
     for buf, _, sem, _ in streams.values():
         pltpu.make_async_copy(
             buf.at[pl.ds(0, n_tok - 1)], buf.at[pl.ds(0, n_tok - 1)], sem
@@ -370,8 +381,8 @@
                 pltpu.VMEM((n_tok, depth, head_cols), bf16),
                 pltpu.VMEM((n_tok, depth, 2 * HD), bf16),
                 pltpu.VMEM((n_tok, depth, head_cols), bf16),
-                pltpu.VMEM((n_tok,) + cache_keys.shape[1:], bf16),
-                pltpu.VMEM((n_tok,) + cache_keys.shape[1:], bf16),
+                pltpu.VMEM((n_tok, 2) + cache_keys.shape[1:], bf16),
+                pltpu.VMEM((n_tok, 2) + cache_keys.shape[1:], bf16),
                 pltpu.VMEM((n_head, rows, width), bf16),
                 pltpu.VMEM(paged, bf16),
                 pltpu.VMEM(paged, bf16),
@@ -383,16 +394,16 @@
                 pltpu.VMEM((rows, HD), jnp.float32),
                 pltpu.VMEM((rows, head_cols), bf16),
                 pltpu.SMEM((pages,), jnp.int32),
-                dma((7,)),
+                dma((9,)),
                 dma((n_head,)),
                 dma((n_tok,)),
                 dma((n_tok,)),
                 dma((n_tok,)),
-                dma((2,)),
+                dma,
                 dma((n_head - 1,)),
                 dma,
                 dma((3,)),
-                dma((2,)),
+                dma,
                 dma((n_head - 1,)),
             ],
             compiler_params=pltpu.CompilerParams(collective_id=0, has_side_effects=True),

time: 84.5 us -> 79.4 us (0.940)
  Pallas kernels: 79.7 us -> 74.7 us
    pallas_call x1, Pallas kernels: 79.7 us -> 74.7 us  [shards(): pl.pallas_call(functools.partial(kernel, n_tok, n_head), out_shape=(jax.S...]
where the time goes in v3:
time: 79.4 us; the launch traced here: 79.2 us
  Pallas kernels  74.7 us (94%)
  local copies, waits for them, and re-layouts  3.19 us (4%)
  between operations  1.3 us (2%)
    pallas_call x1, Pallas kernels, shards(): pl.pallas_call(functools.partial(kernel, n_tok, n_head), out_shape=(jax.S...  74.7 us
    unnamed x7, local copies, waits for them, and re-layouts  3.19 us

profile of v3, /device:TPU:1, one launch (start us, length us, event | category | flops | bytes accessed | tf_op | source)
XLA Modules:
  0.0 79.2 jit_solution(11900074338414792078)
XLA Ops:
  1.3 74.7 %shard_map.121 = (bf16[128,384]{1,0:T(8,128)(2,1)}, bf16[32,16,128]{2,1,0:T(8,128)(2,1)}, bf16[32,16,128]{2,1,0:T(8,128)(2,1)}) custom-call(s32[1]{0:T(128)S(6)} %copy.16.len_ref, s32[1,32]{1,0:T(1,128)} %page_ref.1, bf16[3072]{0:T(1024)(128)(2,1)} %gain_ref.1, bf16[128,384]{1,0:T(8,128)(2,1)} %tok_in.1, bf16[48,384]{1,0:T(8,128)(2,1)} %wq_in.1, ...), custom_call_target="tpu_custom_call" | custom-call | tf_op jit(solution)/shard_map/pallas_call | solution.py:370
  76.0 0.0 copy-start.1
  76.0 1.6 %copy.17 = bf16[128,384]{1,0:T(8,128)(2,1)} copy(bf16[128,384]{1,0:T(8,128)(2,1)} %get-tuple-element.6) | data formatting | bytes 196608
  77.5 0.0 copy-done.1
  77.6 0.0 copy-start
  77.6 0.7 copy.18
  78.2 0.3 copy-done
  78.5 0.7 copy.19
Async XLA Ops:
  76.0 1.6 %copy-start.1 = (bf16[32,16,128]{2,1,0:T(8,128)(2,1)S(1)}, bf16[32,16,128]{2,1,0:T(8,128)(2,1)}, u32[]{:S(2)}) copy-start(bf16[32,16,128]{2,1,0:T(8,128)(2,1)} %get-tuple-element.7) | copy-start | bytes 393220
  77.6 1.0 %copy-start = (bf16[32,16,128]{2,1,0:T(8,128)(2,1)S(1)}, bf16[32,16,128]{2,1,0:T(8,128)(2,1)}, u32[]{:S(2)}) copy-start(bf16[32,16,128]{2,1,0:T(8,128)(2,1)} %get-tuple-element.8) | copy-start | bytes 393220
